TPU v7x, 32 devices: a whole 2x2x4 slice. The times are simulated.
32 devices in a mesh: gx: 4 (over y, core), gy: 8 (over z, x).
Axes of the slice: x: 2, y: 2, z: 4, core: 2. Of those that a mesh axis runs over, the one named last changes fastest.
Arguments:
- a_tiles: bfloat16 [4, 8, 16, 27, 128, 128], P('gx', 'gy'), may hold values from -0.5 to 0.5
- p_tiles: bfloat16 [4, 8, 16, 128, 128], P('gx', 'gy'), may hold values from -1.5 to 1.5
- neighbours: int32 [4, 8, 16, 27], P('gx', 'gy'), may hold values from 0 to 143, as said below
- groups: int32 [4, 8, 16, 27], P('gx', 'gy'), may hold values from 0 to 7
- slots: int32 [4, 8, 16, 8], P('gx', 'gy'), may hold values from 0 to 26
- aggregates: int32 [4, 8, 16], P('gx', 'gy'), may hold values from 0 to 31, as said below
Outputs:
- coarse_tiles: float32 [4, 8, 4, 27, 128, 128], P('gx', 'gy')
Inputs may be any that keep to these rules, and one draw needn't show every extreme that they name: `neighbours`: tile k of a fine row on device (x, y) names row q % 16 of device (x + q // 48 - 1, y + (q // 16) % 3 - 1), which is always on the mesh; tile 0 names the row itself. The owner of aggregate g is gy index g // 4, as its coarse row g % 4. At most 4 fine rows of one device have aggregates with one owner; in every slab one owner gets exactly 4 from every device of the slab.
All inputs are finite; a program needn't handle non-finite values.
Results may differ from a plain program's by a relative error of at most 0.005.
Values may be sent and summed in bfloat16 or wider, within the bound.
A program may use at most 128 MiB of HBM per device.

v0:
```python
import jax
import jax.numpy as jnp
from jax import lax
from jax.sharding import PartitionSpec as P

KC = 27
AGG = 4


def extended(block, sides, width):
    for axis, dim in sides:
        count = lax.axis_size(axis)
        forward = [(i, i + 1) for i in range(count - 1)]
        backward = [(target, source) for source, target in forward]
        low = lax.ppermute(
            lax.slice_in_dim(block, block.shape[dim] - width, None, axis=dim), axis, forward
        )
        high = lax.ppermute(lax.slice_in_dim(block, 0, width, axis=dim), axis, backward)
        block = jnp.concatenate([low, block, high], axis=dim)
    return block


def shards(a_tiles, p_tiles, neighbours, groups, slots, aggregates):
    row_count = a_tiles.shape[2]
    tile_size = a_tiles.shape[-1]
    touched = slots.shape[-1]
    owner_count = lax.axis_size("gy")
    row_cap = (2 * row_count + owner_count - 1) // owner_count
    slot_total = owner_count * row_cap
    coarse_rows = row_count // AGG
    a_local = a_tiles[0, 0]
    p_local = p_tiles[0, 0]
    column_local = neighbours[0, 0]
    group_local = groups[0, 0]
    slot_local = slots[0, 0]
    aggregate_local = aggregates[0, 0]
    padded = extended(p_tiles, (("gx", 0), ("gy", 1)), 1)
    p_table = padded.reshape(9 * row_count, tile_size, tile_size)

    def one_row(inputs):
        a_row, column_row, group_row, p_row = inputs
        far_tiles = jnp.take(p_table, column_row, axis=0)
        products = jnp.einsum("kab,kbc->kac", a_row, far_tiles, preferred_element_type=jnp.float32)
        picker = (group_row[:, None] == jnp.arange(touched, dtype=jnp.int32)[None, :]).astype(
            jnp.float32
        )
        summed = jnp.einsum(
            "kf,kac->fac", picker, products, precision=lax.Precision.HIGHEST
        ).astype(jnp.bfloat16)
        return jnp.einsum("ba,fbc->fac", p_row, summed, preferred_element_type=jnp.float32).astype(
            jnp.bfloat16
        )

    partials = lax.map(one_row, (a_local, column_local, group_local, p_local))
    owners = aggregate_local // coarse_rows
    local_row = aggregate_local % coarse_rows
    indices = jnp.arange(row_count, dtype=jnp.int32)
    same_owner = owners[:, None] == owners[None, :]
    earlier = indices[:, None] > indices[None, :]
    ranking = jnp.sum((same_owner & earlier).astype(jnp.int32), axis=1)
    position = owners * row_cap + ranking
    selector = jnp.arange(slot_total, dtype=jnp.int32)[:, None] == position[None, :]
    meta_ints = jnp.concatenate([(local_row + 1)[:, None], slot_local], axis=1)
    meta_sent = jnp.dot(selector.astype(jnp.int32), meta_ints)
    send_tiles = jnp.einsum(
        "sr,rfab->sfab", selector.astype(jnp.bfloat16), partials, preferred_element_type=jnp.float32
    ).astype(jnp.bfloat16)
    recv_contrib, recv_meta = (
        lax.all_to_all(send_tiles, "gy", split_axis=0, concat_axis=0, tiled=True),
        lax.all_to_all(meta_sent, "gy", split_axis=0, concat_axis=0, tiled=True),
    )
    recv_row = recv_meta[:, 0] - 1
    segment_ids = jnp.where(
        recv_row[:, None] >= 0, recv_row[:, None] * KC + recv_meta[:, 1:], coarse_rows * KC
    )
    flat_contrib = recv_contrib.reshape(slot_total * touched, tile_size, tile_size).astype(
        jnp.float32
    )
    coarse = jax.ops.segment_sum(
        flat_contrib, segment_ids.reshape(-1), num_segments=coarse_rows * KC + 1
    )
    coarse = coarse[: coarse_rows * KC]
    return coarse.reshape(1, 1, coarse_rows, KC, tile_size, tile_size)


def solution(mesh):
    return jax.shard_map(
        shards,
        mesh=mesh,
        in_specs=(
            P("gx", "gy", None, None, None, None),
            P("gx", "gy", None, None, None),
            P("gx", "gy", None, None),
            P("gx", "gy", None, None),
            P("gx", "gy", None, None),
            P("gx", "gy", None),
        ),
        out_specs=P("gx", "gy", None, None, None, None),
        check_vma=False,
    )
```

profile of v0, /device:TPU:0, one launch (start us, length us, event | category | flops | bytes accessed | tf_op | source)
XLA Modules:
  0.0 539.2 jit_solution(3211491766969522119)
XLA Ops:
  0.0 2.4 collective-permute-start
  5.3 3.2 collective-permute-done.1
  8.6 3.5 collective-permute-start.2
  17.2 8.0 %all-to-all-start = ((s32[8,4,9]{2,1,0:T(4,128)}), s32[8,4,9]{2,1,0:T(4,128)S(1)}, u32[]{:S(2)}, u32[]{:S(2)}) async-start(s32[8,4,9]{2,1,0:T(4,128)} %bitcast.13), calls=%async_computation | async-start | bytes 32768 | tf_op jit(solution)/shard_map/all_to_all | solution.py:70
  25.2 51.0 %collective-permute-done.2 = bf16[3,1,16,128,128]{4,3,2,1,0:T(8,128)(2,1)S(1)} collective-permute-done((bf16[3,1,16,128,128]{4,3,2,1,0:T(8,128)(2,1)S(1)}, bf16[3,1,16,128,128]{4,3,2,1,0:T(8,128)(2,1)S(1)}, u32[]{:S(2)}, u32[]{:S(2)}) %collective-permute-start.2) | collective-permute-done | bytes 1572896 | tf_op jit(solution)/shard_map/ppermute | solution.py:15
  76.2 3.6 pad_maximum_fusion
  79.7 164.5 %while.10 = (s32[]{:T(128)}, bf16[16,8,128,128]{2,3,1,0:T(8,128)(2,1)}, s32[16,27]{1,0:T(8,128)}, bf16[16,27,128,128]{3,2,1,0:T(8,128)(2,1)}, s32[16,27]{1,0:T(8...) while((s32[]{:T(128)}, bf16[16,8,128,128]{2,3,1,0:T(8,128)(2,1)}, ...), condition=%wide.region_2.3_spmd, body=%wide.region_1.2_spmd.sunk | while | flops 189973952 | bytes 7903735 | solution.py:54
  80.4 3.1 gather_fusion
  86.5 1.7 fusion.58
  90.7 3.1 gather_fusion
  96.8 1.7 fusion.58
  101.0 3.1 gather_fusion
  107.1 1.7 fusion.58
  111.2 3.1 gather_fusion
  117.3 1.7 fusion.58
  121.5 3.1 gather_fusion
  127.6 1.7 fusion.58
  131.8 3.1 gather_fusion
  137.9 1.7 fusion.58
  142.1 3.1 gather_fusion
  148.2 1.7 fusion.58
  152.4 3.1 gather_fusion
  158.5 1.7 fusion.58
  162.7 3.1 gather_fusion
  168.8 1.7 fusion.58
  170.5 1.8 fusion.59
  173.0 3.1 gather_fusion
  179.1 1.7 fusion.58
  183.3 3.1 gather_fusion
  189.4 1.7 fusion.58
  193.5 3.1 gather_fusion
  199.6 1.7 fusion.58
  203.8 3.1 gather_fusion
  209.9 1.7 fusion.58
  214.1 3.1 gather_fusion
  224.4 3.1 gather_fusion
  230.5 1.7 fusion.58
  234.7 3.1 gather_fusion
  240.8 1.7 fusion.58
  244.3 6.7 %copy.24 = bf16[16,8,128,128]{3,0,2,1:T(8,128)(2,1)} copy(bf16[16,8,128,128]{2,3,1,0:T(8,128)(2,1)} %get-tuple-element.42) | data formatting | bytes 8388608 | tf_op jit(solution)/shard_map/while | solution.py:54
  251.0 7.8 %convolution_convert_fusion.1 = bf16[32,8,128,128]{3,0,2,1:T(8,128)(2,1)} fusion(bf16[16,8,128,128]{3,0,2,1:T(8,128)(2,1)} %copy.24, s32[16]{0:T(128)S(1)} %multiply_add_fusion), kind=kOutput, calls=%fused_computation.32 | convolution fusion | flops 138412544 | bytes 12582976 | tf_op jit(solution)/shard_map/sr,rfab->sfab/dot_general | solution.py:65
  258.8 9.8 %copy.25 = bf16[32,8,128,128]{3,2,1,0:T(8,128)(2,1)} copy(bf16[32,8,128,128]{3,0,2,1:T(8,128)(2,1)} %convolution_convert_fusion.1) | data formatting | bytes 16777216 | tf_op jit(solution)/shard_map/convert_element_type | solution.py:67
  268.6 11.2 %all-to-all-start.1 = ((bf16[32,8,128,128]{3,2,1,0:T(8,128)(2,1)}), bf16[32,8,128,128]{3,2,1,0:T(8,128)(2,1)}, u32[]{:S(2)}, u32[]{:S(2)}) async-start(bf16[32,8,128,128]{3,2,1,0:T(8,128)(2,1)} %copy.25), calls=%async_computation.1 | async-start | bytes 16777216 | tf_op jit(solution)/shard_map/all_to_all | solution.py:69
  280.3 183.7 %all-to-all-done.1 = bf16[32,8,128,128]{3,2,1,0:T(8,128)(2,1)} async-done(((bf16[32,8,128,128]{3,2,1,0:T(8,128)(2,1)}), bf16[32,8,128,128]{3,2,1,0:T(8,128)(2,1)}, u32[]{:S(2)}, u32[]{:S(2)}) %all-to-all-start.1) | async-done | bytes 8388640 | tf_op jit(solution)/shard_map/all_to_all | solution.py:69
  464.0 11.2 %bitcast_convert_fusion = f32[256,128,128]{2,1,0:T(8,128)} fusion(bf16[32,8,128,128]{3,2,1,0:T(8,128)(2,1)} %all-to-all-done.1), kind=kLoop, calls=%fused_computation.31 | loop fusion | flops 4194304 | bytes 25165824 | tf_op jit(solution)/shard_map/convert_element_type | solution.py:76
  475.2 3.8 broadcast_in_dim.45
  479.0 53.3 %scatter_fusion = f32[109,128,128]{2,1,0:T(8,128)} fusion(f32[109,128,128]{2,1,0:T(8,128)} %broadcast_in_dim.45, s32[256]{0:T(256)S(1)} %reshape.186, f32[256,128,128]{2,1,0:T(8,128)} %bitcast_convert_fusion), kind=kCustom, calls=%fused_computation.1 | custom fusion | flops 4194304 | bytes 50332672 | tf_op jit(solution)/shard_map/scatter-add | solution.py:79
  532.3 6.9 %slice.16 = f32[108,128,128]{2,1,0:T(8,128)} slice(f32[109,128,128]{2,1,0:T(8,128)} %scatter_fusion), slice={[0:108], [0:128], [0:128]} | slice | bytes 14155776 | tf_op jit(solution)/shard_map/slice | solution.py:82
  (114 shorter events, 95.7 us)
Async XLA Ops:
  0.0 4.1 collective-permute-start
  2.4 6.1 %collective-permute-start.1 = (bf16[1,1,16,128,128]{4,3,2,1,0:T(8,128)(2,1)}, bf16[1,1,16,128,128]{4,3,2,1,0:T(8,128)(2,1)S(1)}, u32[]{:S(2)}, u32[]{:S(2)}) collective-permute-start(bf16[1,1,16,128,128]{4,3,2,1,0:T(8,128)(2,1)} %param.9), channel_id=1, source_target_pairs={{8,0},{16,8},{24,16},{9,1},{17,9},{25,17},{10,2},{18,10},{26,18},{... | collective-permute-start | bytes 1572872 | tf_op jit(solution)/shard_map/ppermute | solution.py:18
  8.6 67.5 %collective-permute-start.2 = (bf16[3,1,16,128,128]{4,3,2,1,0:T(8,128)(2,1)S(1)}, bf16[3,1,16,128,128]{4,3,2,1,0:T(8,128)(2,1)S(1)}, u32[]{:S(2)}, u32[]{:S(2)}) collective-permute-start(bf16[3,1,16,128,128]{4,3,2,1,0:T(8,128)(2,1)S(1)} %constant_dynamic-update-slice_fusion), channel_id=1, source_target_pairs={{0,1},{1,2},{2,3},{3,4},{4,5},{5,6},{6,7},{8,9},{9,10},{10,11},{11... | collective-permute-start | bytes 4718600 | tf_op jit(solution)/shard_map/ppermute | solution.py:15
  12.1 64.0 %collective-permute-start.3 = (bf16[3,1,16,128,128]{4,3,2,1,0:T(8,128)(2,1)S(1)}, bf16[3,1,16,128,128]{4,3,2,1,0:T(8,128)(2,1)}, u32[]{:S(2)}, u32[]{:S(2)}) collective-permute-start(bf16[3,1,16,128,128]{4,3,2,1,0:T(8,128)(2,1)S(1)} %constant_dynamic-update-slice_fusion), channel_id=1, source_target_pairs={{1,0},{2,1},{3,2},{4,3},{5,4},{6,5},{7,6},{9,8},{10,9},{11,10},{12... | collective-permute-start | bytes 4718600 | tf_op jit(solution)/shard_map/ppermute | solution.py:18
  17.2 251.5 %all-to-all-start = ((s32[8,4,9]{2,1,0:T(4,128)}), s32[8,4,9]{2,1,0:T(4,128)S(1)}, u32[]{:S(2)}, u32[]{:S(2)}) async-start(s32[8,4,9]{2,1,0:T(4,128)} %bitcast.13), calls=%async_computation | async-start | bytes 32768 | tf_op jit(solution)/shard_map/all_to_all | solution.py:70
  268.6 195.4 %all-to-all-start.1 = ((bf16[32,8,128,128]{3,2,1,0:T(8,128)(2,1)}), bf16[32,8,128,128]{3,2,1,0:T(8,128)(2,1)}, u32[]{:S(2)}, u32[]{:S(2)}) async-start(bf16[32,8,128,128]{3,2,1,0:T(8,128)(2,1)} %copy.25), calls=%async_computation.1 | async-start | bytes 16777216 | tf_op jit(solution)/shard_map/all_to_all | solution.py:69
where the time goes:
time: 544 us; the launch traced here: 539 us
  waiting for transfers between devices  238 us (44%)
  other arithmetic  93 us (17%)
  matrix products  91.1 us (17%)
  local copies, waits for them, and re-layouts  88.6 us (16%)
  starting transfers between devices  27.8 us (5%)
    all_to_all x1, waiting for transfers between devices, shards(): lax.all_to_all(send_tiles, 'gy', split_axis=0, concat_axis=0, tiled=True)  184 us
    scatter-add x1, other arithmetic, shards(): jax.ops.segment_sum(flat_contrib, segment_ids.reshape(-1), num_segments=c...  53.3 us
    ppermute x2, waiting for transfers between devices, extended(): lax.ppermute(lax.slice_in_dim(block, block.shape[dim] - width, None, axis...  51.4 us
    gather x16, local copies, waits for them, and re-layouts, one_row(): far_tiles = jnp.take(p_table, column_row, axis=0)  48.9 us
    dot_general x16, matrix products, one_row(): jnp.einsum('kf,kac->fac', picker, products, precision=lax.Precision.HIGHEST)  28 us
    dot_general x16, matrix products, one_row(): jnp.einsum('ba,fbc->fac', p_row, summed, preferred_element_type=jnp.float32)  27.7 us
    dot_general x16, matrix products, one_row(): jnp.einsum('kab,kbc->kac', a_row, far_tiles, preferred_element_type=jnp.f...  26 us
    and x16, other arithmetic, one_row(): far_tiles = jnp.take(p_table, column_row, axis=0)  11.3 us
  transfers between devices with their start and end apart: 6, of which 4 were waited for; matrix products, arithmetic and copies ran while one was open for 37% of the time, Pallas kernels for 0%

commit v1 on v0

--- a/solution.py
+++ b/solution.py
@@ -5,6 +5,22 @@
 
 KC = 27
 AGG = 4
+
+
+def swapped_with_each(shard, axis, split, join):
+    ways, here = (lax.axis_size(axis), lax.axis_index(axis))
+    width = shard.shape[split] // ways
+    shape = list(shard.shape)
+    shape[split] = width
+    height = shape[join]
+    shape[join] = height * ways
+    full = jnp.zeros(shape, shard.dtype)
+    for mask in range(ways):
+        part = lax.dynamic_slice_in_dim(shard, (here ^ mask) * width, width, axis=split)
+        if mask:
+            part = lax.ppermute(part, axis, [(d, d ^ mask) for d in range(ways)])
+        full = lax.dynamic_update_slice_in_dim(full, part, (here ^ mask) * height, axis=join)
+    return full
 
 
 def extended(block, sides, width):
@@ -66,7 +82,7 @@
         "sr,rfab->sfab", selector.astype(jnp.bfloat16), partials, preferred_element_type=jnp.float32
     ).astype(jnp.bfloat16)
     recv_contrib, recv_meta = (
-        lax.all_to_all(send_tiles, "gy", split_axis=0, concat_axis=0, tiled=True),
+        swapped_with_each(send_tiles, "gy", 0, 0),
         lax.all_to_all(meta_sent, "gy", split_axis=0, concat_axis=0, tiled=True),
     )
     recv_row = recv_meta[:, 0] - 1

time: 544 us -> 558 us (1.026)
  the two profiles are of different devices: /device:TPU:0 before, /device:TPU:16 now
where the time goes in v1:
time: 558 us; the launch traced here: 553 us
  waiting for transfers between devices  227 us (41%)
  local copies, waits for them, and re-layouts  104 us (19%)
  other arithmetic  91.7 us (16%)
  matrix products  86.5 us (16%)
  blocking collectives  24.9 us (4%)
  starting transfers between devices  19.1 us (3%)
    ppermute x7, waiting for transfers between devices, swapped_with_each(): part = lax.ppermute(part, axis, [(d, d ^ mask) for d in range(ways)])  158 us
    ppermute x2, waiting for transfers between devices, extended(): lax.ppermute(lax.slice_in_dim(block, block.shape[dim] - width, None, axis...  59.4 us
    scatter-add x1, other arithmetic, shards(): jax.ops.segment_sum(flat_contrib, segment_ids.reshape(-1), num_segments=c...  52.6 us
    gather x16, local copies, waits for them, and re-layouts, one_row(): far_tiles = jnp.take(p_table, column_row, axis=0)  48.9 us
    dot_general x16, matrix products, one_row(): jnp.einsum('kf,kac->fac', picker, products, precision=lax.Precision.HIGHEST)  28 us
    dot_general x16, matrix products, one_row(): jnp.einsum('ba,fbc->fac', p_row, summed, preferred_element_type=jnp.float32)  27.6 us
    dot_general x16, matrix products, one_row(): jnp.einsum('kab,kbc->kac', a_row, far_tiles, preferred_element_type=jnp.f...  26.1 us
    all_to_all x1, blocking collectives, shards(): lax.all_to_all(meta_sent, 'gy', split_axis=0, concat_axis=0, tiled=True)  24.9 us
  transfers between devices with their start and end apart: 11, of which 9 were waited for; matrix products, arithmetic and copies ran while one was open for 4% of the time, Pallas kernels for 0%

profile of v1, /device:TPU:16, one launch (start us, length us, event | category | flops | bytes accessed | tf_op | source)
XLA Modules:
  0.0 553.1 jit_solution(5568995152177312878)
XLA Ops:
  0.0 1.8 collective-permute-start
  4.6 2.4 collective-permute-done.1
  7.1 3.4 collective-permute-start.2
  10.5 3.3 collective-permute-start.3
  15.5 59.1 %collective-permute-done.2 = bf16[3,1,16,128,128]{4,3,2,1,0:T(8,128)(2,1)S(1)} collective-permute-done((bf16[3,1,16,128,128]{4,3,2,1,0:T(8,128)(2,1)S(1)}, bf16[3,1,16,128,128]{4,3,2,1,0:T(8,128)(2,1)S(1)}, u32[]{:S(2)}, u32[]{:S(2)}) %collective-permute-start.2) | collective-permute-done | bytes 1572896 | tf_op jit(solution)/shard_map/ppermute | solution.py:31
  74.5 6.4 %collective-permute-done.3 = bf16[3,1,16,128,128]{4,3,2,1,0:T(8,128)(2,1)} collective-permute-done((bf16[3,1,16,128,128]{4,3,2,1,0:T(8,128)(2,1)S(1)}, bf16[3,1,16,128,128]{4,3,2,1,0:T(8,128)(2,1)}, u32[]{:S(2)}, u32[]{:S(2)}) %collective-permute-start.3) | collective-permute-done | bytes 1572896 | tf_op jit(solution)/shard_map/ppermute | solution.py:34
  80.9 3.6 pad_maximum_fusion
  84.5 164.4 %while.10 = (s32[]{:T(128)}, bf16[16,8,128,128]{2,3,1,0:T(8,128)(2,1)}, s32[16,27]{1,0:T(8,128)}, bf16[16,27,128,128]{3,2,1,0:T(8,128)(2,1)}, s32[16,27]{1,0:T(8...) while((s32[]{:T(128)}, bf16[16,8,128,128]{2,3,1,0:T(8,128)(2,1)}, ...), condition=%wide.region_2.3_spmd, body=%wide.region_1.2_spmd.sunk | while | flops 189973952 | bytes 7903735 | solution.py:70
  85.2 3.1 gather_fusion
  95.4 3.1 gather_fusion
  105.7 3.1 gather_fusion
  116.0 3.1 gather_fusion
  126.2 3.1 gather_fusion
  136.5 3.1 gather_fusion
  142.6 1.7 fusion.58
  146.8 3.1 gather_fusion
  157.1 3.1 gather_fusion
  163.2 1.7 fusion.58
  167.4 3.1 gather_fusion
  177.7 3.1 gather_fusion
  187.9 3.1 gather_fusion
  198.2 3.1 gather_fusion
  204.3 1.7 fusion.58
  206.1 1.8 fusion.59
  208.5 3.1 gather_fusion
  218.8 3.1 gather_fusion
  224.9 1.7 fusion.58
  229.1 3.1 gather_fusion
  235.2 1.7 fusion.58
  239.3 3.1 gather_fusion
  248.9 6.7 %copy.33 = bf16[16,8,128,128]{3,0,2,1:T(8,128)(2,1)} copy(bf16[16,8,128,128]{2,3,1,0:T(8,128)(2,1)} %get-tuple-element.42) | data formatting | bytes 8388608 | tf_op jit(solution)/shard_map/while | solution.py:70
  255.6 4.6 convolution_convert_fusion.1
  260.3 6.1 %constant_dynamic-slice_fusion.2 = (bf16[4,8,128,128]{3,0,2,1:T(4,128)(2,1)S(1)}, bf16[4,8,128,128]{3,0,2,1:T(4,128)(2,1)S(1)}, bf16[4,8,128,128]{3,0,2,1:T(4,12...) fusion(bf16[32,8,128,128]{3,0,2,1:T(8,128)(2,1)S(1)} %convoluti, ...), kind=kLoop, calls=%fused_computation.62 | loop fusion | bytes 16777248 | tf_op jit(solution)/shard_map/dynamic_slice | solution.py:19
  268.3 24.9 %all_to_all.12 = s32[8,4,9]{2,1,0:T(4,128)S(1)} all-to-all(s32[8,4,9]{2,1,0:T(4,128)S(1)} %bitcast.76), channel_id=1, replica_groups=mesh['gx'=4,'gy'=8] {'gy'}, dimensions={0} | all-to-all | bytes 2304 | tf_op jit(solution)/shard_map/all_to_all | solution.py:86
  296.7 2.5 collective-permute-start.8
  299.2 5.3 broadcast_in_dim.52
  307.1 2.5 copy_dynamic-update-slice_fusion.6
  310.3 2.5 copy_dynamic-update-slice_fusion.5
  312.8 26.1 %collective-permute-done.6 = bf16[4,8,128,128]{3,0,2,1:T(4,128)(2,1)} collective-permute-done((bf16[4,8,128,128]{3,0,2,1:T(4,128)(2,1)}, bf16[4,8,128,128]{3,0,2,1:T(4,128)(2,1)}, u32[]{:S(2)}, u32[]{:S(2)}) %collective-permute-start.6) | collective-permute-done | bytes 1048608 | tf_op jit(solution)/shard_map/ppermute | solution.py:21
  338.8 2.5 copy_dynamic-update-slice_fusion.4
  341.3 69.1 %collective-permute-done.7 = bf16[4,8,128,128]{3,0,2,1:T(4,128)(2,1)S(1)} collective-permute-done((bf16[4,8,128,128]{3,0,2,1:T(4,128)(2,1)}, bf16[4,8,128,128]{3,0,2,1:T(4,128)(2,1)S(1)}, u32[]{:S(2)}, u32[]{:S(2)}) %collective-permute-start.7) | collective-permute-done | bytes 1048608 | tf_op jit(solution)/shard_map/ppermute | solution.py:21
  411.7 21.2 %collective-permute-done.8 = bf16[4,8,128,128]{3,0,2,1:T(4,128)(2,1)S(1)} collective-permute-done((bf16[4,8,128,128]{3,0,2,1:T(4,128)(2,1)}, bf16[4,8,128,128]{3,0,2,1:T(4,128)(2,1)S(1)}, u32[]{:S(2)}, u32[]{:S(2)}) %collective-permute-start.8) | collective-permute-done | bytes 1048608 | tf_op jit(solution)/shard_map/ppermute | solution.py:21
  434.2 22.1 %collective-permute-done.9 = bf16[4,8,128,128]{3,0,2,1:T(4,128)(2,1)S(1)} collective-permute-done((bf16[4,8,128,128]{3,0,2,1:T(4,128)(2,1)S(1)}, bf16[4,8,128,128]{3,0,2,1:T(4,128)(2,1)S(1)}, u32[]{:S(2)}, u32[]{:S(2)}) %collective-permute-start.9) | collective-permute-done | bytes 1048608 | tf_op jit(solution)/shard_map/ppermute | solution.py:21
  457.5 19.8 %collective-permute-done.10 = bf16[4,8,128,128]{3,0,2,1:T(4,128)(2,1)S(1)} collective-permute-done((bf16[4,8,128,128]{3,0,2,1:T(4,128)(2,1)S(1)}, bf16[4,8,128,128]{3,0,2,1:T(4,128)(2,1)S(1)}, u32[]{:S(2)}, u32[]{:S(2)}) %collective-permute-start.10) | collective-permute-done | bytes 1048608 | tf_op jit(solution)/shard_map/ppermute | solution.py:21
  478.5 11.2 %bitcast_convert_fusion = f32[256,128,128]{2,1,0:T(8,128)} fusion(bf16[32,8,128,128]{3,2,1,0:T(8,128)(2,1)} %copy_dynamic-update-slice_fusion), kind=kLoop, calls=%fused_computation.31 | loop fusion | flops 4194304 | bytes 25165824 | tf_op jit(solution)/shard_map/convert_element_type | solution.py:92
  489.8 3.8 broadcast_in_dim.48
  493.6 52.6 %scatter_fusion = f32[109,128,128]{2,1,0:T(8,128)} fusion(f32[109,128,128]{2,1,0:T(8,128)} %broadcast_in_dim.48, s32[256]{0:T(256)S(1)} %reshape.186, f32[256,128,128]{2,1,0:T(8,128)} %bitcast_convert_fusion), kind=kCustom, calls=%fused_computation.1 | custom fusion | flops 4194304 | bytes 50332672 | tf_op jit(solution)/shard_map/scatter-add | solution.py:95
  546.2 6.9 %slice.16 = f32[108,128,128]{2,1,0:T(8,128)} slice(f32[109,128,128]{2,1,0:T(8,128)} %scatter_fusion), slice={[0:108], [0:128], [0:128]} | slice | bytes 14155776 | tf_op jit(solution)/shard_map/slice | solution.py:98
  (138 shorter events, 123.0 us)
Async XLA Ops:
  0.0 3.5 collective-permute-start
  1.8 5.3 collective-permute-start.1
  7.1 67.4 %collective-permute-start.2 = (bf16[3,1,16,128,128]{4,3,2,1,0:T(8,128)(2,1)S(1)}, bf16[3,1,16,128,128]{4,3,2,1,0:T(8,128)(2,1)S(1)}, u32[]{:S(2)}, u32[]{:S(2)}) collective-permute-start(bf16[3,1,16,128,128]{4,3,2,1,0:T(8,128)(2,1)S(1)} %constant_dynamic-update-slice_fusion), channel_id=1, source_target_pairs={{0,1},{1,2},{2,3},{3,4},{4,5},{5,6},{6,7},{8,9},{9,10},{10,11},{11... | collective-permute-start | bytes 4718600 | tf_op jit(solution)/shard_map/ppermute | solution.py:31
  10.5 70.4 %collective-permute-start.3 = (bf16[3,1,16,128,128]{4,3,2,1,0:T(8,128)(2,1)S(1)}, bf16[3,1,16,128,128]{4,3,2,1,0:T(8,128)(2,1)}, u32[]{:S(2)}, u32[]{:S(2)}) collective-permute-start(bf16[3,1,16,128,128]{4,3,2,1,0:T(8,128)(2,1)S(1)} %constant_dynamic-update-slice_fusion), channel_id=1, source_target_pairs={{1,0},{2,1},{3,2},{4,3},{5,4},{6,5},{7,6},{9,8},{10,9},{11,10},{12... | collective-permute-start | bytes 4718600 | tf_op jit(solution)/shard_map/ppermute | solution.py:34
  260.2 6.1 %copy-start.1 = (s32[1,1,16]{2,1,0:T(1,128)S(1)}, s32[1,1,16]{2,1,0:T(1,128)}, u32[]{:S(2)}) copy-start(s32[1,1,16]{2,1,0:T(1,128)} %param.13) | copy-start | bytes 196
  260.2 7.7 %copy-start = (s32[1,1,16,8]{2,3,1,0:T(8,128)S(1)}, s32[1,1,16,8]{2,3,1,0:T(8,128)}, u32[]{:S(2)}) copy-start(s32[1,1,16,8]{2,3,1,0:T(8,128)} %param.12) | copy-start | bytes 1540
  266.3 39.4 %collective-permute-start.4 = (bf16[4,8,128,128]{3,0,2,1:T(4,128)(2,1)}, bf16[4,8,128,128]{3,0,2,1:T(4,128)(2,1)}, u32[]{:S(2)}, u32[]{:S(2)}) collective-permute-start(bf16[4,8,128,128]{3,0,2,1:T(4,128)(2,1)} %get-tuple-element.63), channel_id=1, source_target_pairs={{0,1},{1,0},{2,3},{3,2},{4,5},{5,4},{6,7},{7,6},{8,9},{9,8},{10,11... | collective-permute-start | bytes 3145736 | tf_op jit(solution)/shard_map/ppermute | solution.py:21
  266.3 43.2 %collective-permute-start.5 = (bf16[4,8,128,128]{3,0,2,1:T(4,128)(2,1)}, bf16[4,8,128,128]{3,0,2,1:T(4,128)(2,1)}, u32[]{:S(2)}, u32[]{:S(2)}) collective-permute-start(bf16[4,8,128,128]{3,0,2,1:T(4,128)(2,1)} %get-tuple-element.62), channel_id=1, source_target_pairs={{0,2},{1,3},{2,0},{3,1},{4,6},{5,7},{6,4},{7,5},{8,10},{9,11},{10,... | collective-permute-start | bytes 3145736 | tf_op jit(solution)/shard_map/ppermute | solution.py:21
  293.4 45.4 %collective-permute-start.6 = (bf16[4,8,128,128]{3,0,2,1:T(4,128)(2,1)}, bf16[4,8,128,128]{3,0,2,1:T(4,128)(2,1)}, u32[]{:S(2)}, u32[]{:S(2)}) collective-permute-start(bf16[4,8,128,128]{3,0,2,1:T(4,128)(2,1)} %get-tuple-element.61), channel_id=1, source_target_pairs={{0,3},{1,2},{2,1},{3,0},{4,7},{5,6},{6,5},{7,4},{8,11},{9,10},{10,... | collective-permute-start | bytes 3145736 | tf_op jit(solution)/shard_map/ppermute | solution.py:21
  295.3 115.1 %collective-permute-start.7 = (bf16[4,8,128,128]{3,0,2,1:T(4,128)(2,1)}, bf16[4,8,128,128]{3,0,2,1:T(4,128)(2,1)S(1)}, u32[]{:S(2)}, u32[]{:S(2)}) collective-permute-start(bf16[4,8,128,128]{3,0,2,1:T(4,128)(2,1)} %get-tuple-element.60), channel_id=1, source_target_pairs={{0,4},{1,5},{2,6},{3,7},{4,0},{5,1},{6,2},{7,3},{8,12},{9,13},{10,... | collective-permute-start | bytes 3145736 | tf_op jit(solution)/shard_map/ppermute | solution.py:21
  296.7 136.2 %collective-permute-start.8 = (bf16[4,8,128,128]{3,0,2,1:T(4,128)(2,1)}, bf16[4,8,128,128]{3,0,2,1:T(4,128)(2,1)S(1)}, u32[]{:S(2)}, u32[]{:S(2)}) collective-permute-start(bf16[4,8,128,128]{3,0,2,1:T(4,128)(2,1)} %get-tuple-element.59), channel_id=1, source_target_pairs={{0,5},{1,4},{2,7},{3,6},{4,1},{5,0},{6,3},{7,2},{8,13},{9,12},{10,... | collective-permute-start | bytes 3145736 | tf_op jit(solution)/shard_map/ppermute | solution.py:21
  305.7 150.5 %collective-permute-start.9 = (bf16[4,8,128,128]{3,0,2,1:T(4,128)(2,1)S(1)}, bf16[4,8,128,128]{3,0,2,1:T(4,128)(2,1)S(1)}, u32[]{:S(2)}, u32[]{:S(2)}) collective-permute-start(bf16[4,8,128,128]{3,0,2,1:T(4,128)(2,1)S(1)} %get-tuple-element.58), channel_id=1, source_target_pairs={{0,6},{1,7},{2,4},{3,5},{4,2},{5,3},{6,0},{7,1},{8,14},{9,15},{10,... | collective-permute-start | bytes 3145736 | tf_op jit(solution)/shard_map/ppermute | solution.py:21
  309.6 167.7 %collective-permute-start.10 = (bf16[4,8,128,128]{3,0,2,1:T(4,128)(2,1)S(1)}, bf16[4,8,128,128]{3,0,2,1:T(4,128)(2,1)S(1)}, u32[]{:S(2)}, u32[]{:S(2)}) collective-permute-start(bf16[4,8,128,128]{3,0,2,1:T(4,128)(2,1)S(1)} %get-tuple-element.57), channel_id=1, source_target_pairs={{0,7},{1,6},{2,5},{3,4},{4,3},{5,2},{6,1},{7,0},{8,15},{9,14},{10,... | collective-permute-start | bytes 3145736 | tf_op jit(solution)/shard_map/ppermute | solution.py:21
